TPU v7x, 256 devices: a whole 4x4x8 slice. The times are simulated.
256 devices in a mesh: train: 16 (over y_lo, z), test: 16 (over x, y_hi, core).
Axes of the slice: x: 4, y: 4 (y_hi: 2, y_lo: 2; y = y_hi * 2 + y_lo), z: 8, core: 2. Of those that a mesh axis runs over, the one named last changes fastest.
Arguments:
- query_out: bfloat16 [4096, 3584], P('train', 'test'), may hold values from -16 to 16, as said below
- query_in: bfloat16 [4096, 3584], P('train', 'test'), may hold values from -6 to 6
- passage_out: bfloat16 [4096, 3584], P('train', 'test'), may hold values from -16 to 16, as said below
- passage_in_sum: bfloat16 [4096, 3584], P('train', 'test'), may hold values from -192 to 192
- passage_len: int32 [4096], P('train'), may hold values from 16 to 512
- positive: int32 [4096], P('train'), may hold values from 0 to 4095
- proj_in: bfloat16 [3584, 64], P('test'), may hold values from -0.09375 to 0.09375
- proj_out: bfloat16 [3584, 64], P('test'), may hold values from -0.09375 to 0.09375
- test_grads: bfloat16 [16384, 4096], P(('test', 'train')), may hold values from -6 to 6
Outputs:
- scores: float32 [4096, 16384], P('train', 'test')
Inputs may be any that keep to these rules, and one draw needn't show every extreme that they name: `query_out`: entries stay within the range. `passage_out`: entries stay within the range.
All inputs are finite; a program needn't handle non-finite values.
Results may differ from a plain program's by a relative error of at most 0.0034.
Values may be sent and summed in bfloat16 or wider, within the bound.
A program may use at most 64 MiB of HBM per device.

v0:
```python
import math
import jax
import jax.numpy as jnp
from jax import lax
from jax.sharding import PartitionSpec as P

D = 3584


def copy_for_each(value, axis):
    copies = jnp.broadcast_to(value, (lax.axis_size(axis), *value.shape))
    return lax.all_to_all(copies, axis, split_axis=0, concat_axis=0, tiled=True)


def laid_out(blocks, dim):
    dims = list(blocks.shape[1:])
    dims[dim] *= blocks.shape[0]
    return jnp.moveaxis(blocks, 0, dim).reshape(dims)


def gathered_copies(value, axis, dim):
    blocks = copy_for_each(value, axis)
    return laid_out(blocks, dim)


def taken_together(value, axis):
    return copy_for_each(value, axis).max(axis=0)


def over_copies(value, axis):
    everything = copy_for_each(value, axis)
    return jnp.sum(everything, axis=0)


def split_up(value, dim, count):
    dims = value.shape
    blocks = value.reshape(*dims[:dim], count, dims[dim] // count, *dims[dim + 1 :])
    return jnp.moveaxis(blocks, dim, 0)


def summed_on_arrival(value, axis, dim):
    count = lax.axis_size(axis)
    blocks = lax.all_to_all(split_up(value, dim, count), axis, 0, 0, tiled=True)
    return jnp.sum(blocks, axis=0)


def in_one(arrays, axis):
    ends = [0]
    for a in arrays:
        ends.append(ends[-1] + a.size)
    so_far = lax.psum(jnp.concatenate([a.ravel() for a in arrays]), axis)
    return tuple((so_far[b:e].reshape(a.shape) for a, b, e in zip(arrays, ends, ends[1:])))


def local(
    query_out,
    query_in,
    passage_out,
    passage_in_sum,
    passage_len,
    positive,
    proj_in,
    proj_out,
    test_grads,
):
    rank_size = proj_in.shape[1]
    logit_scale = 1.0 / math.sqrt(D)
    whole_pass = gathered_copies(passage_out, "train", 0)
    pass_block = lax.all_to_all(whole_pass, "test", split_axis=0, concat_axis=1, tiled=True)
    query_full = lax.all_gather(query_out, "test", axis=1, tiled=True)
    proj_full = gathered_copies(proj_out, "test", 0).astype(jnp.float32)
    block_logits = (
        lax.dot_general(
            query_full, pass_block, (((1,), (1,)), ((), ())), preferred_element_type=jnp.float32
        )
        * logit_scale
    )
    block_cols = block_logits.shape[1]
    block_top = taken_together(jnp.max(block_logits, axis=1), "test")
    block_exp = jnp.exp(block_logits - block_top[:, None])
    block_sum = over_copies(jnp.sum(block_exp, axis=1), "test")
    first_col = lax.axis_index("test") * block_cols
    col_index = lax.broadcasted_iota(jnp.int32, block_logits.shape, 1) + first_col
    block_hit = (col_index == positive[:, None]).astype(jnp.float32)
    block_grad = (block_exp / block_sum[:, None] - block_hit).astype(jnp.bfloat16)
    query_partial = (
        jnp.dot(block_grad, pass_block, preferred_element_type=jnp.float32) * logit_scale
    )
    out_query = jnp.dot(query_partial, proj_full, precision=lax.Precision.HIGHEST)
    pass_partial = (
        lax.dot_general(
            block_grad, query_full, (((0,), (0,)), ((), ())), preferred_element_type=jnp.float32
        )
        * logit_scale
    )
    pass_small = jnp.dot(pass_partial, proj_full, precision=lax.Precision.HIGHEST)
    padded = jnp.zeros((whole_pass.shape[0], rank_size), jnp.float32)
    padded = lax.dynamic_update_slice_in_dim(padded, pass_small, first_col, 0)
    out_pass = summed_on_arrival(padded, "train", 0)
    act_query = jnp.dot(query_in, proj_in, preferred_element_type=jnp.float32)
    act_pass = jnp.dot(passage_in_sum, proj_in, preferred_element_type=jnp.float32)
    act_query, act_pass, out_query, out_pass = in_one(
        (act_query, act_pass, out_query, out_pass), "test"
    )
    act_pass = act_pass / passage_len[:, None].astype(jnp.float32)
    stacked = jnp.stack((act_query, act_pass, out_query, out_pass), axis=1)
    row_count = stacked.shape[0]
    outer = (
        stacked[:, 0, :, None] * stacked[:, 2, None, :]
        + stacked[:, 1, :, None] * stacked[:, 3, None, :]
    )
    train_grads = outer.reshape(row_count, rank_size * rank_size).astype(jnp.bfloat16)
    return lax.dot_general(
        train_grads,
        lax.all_gather(test_grads, "train", axis=0, tiled=True),
        (((1,), (1,)), ((), ())),
        preferred_element_type=jnp.float32,
    )


def solution(mesh):
    return jax.shard_map(
        local,
        mesh=mesh,
        in_specs=(
            P("train", "test"),
            P("train", "test"),
            P("train", "test"),
            P("train", "test"),
            P("train"),
            P("train"),
            P("test", None),
            P("test", None),
            P(("test", "train"), None),
        ),
        out_specs=P("train", "test"),
        check_vma=False,
    )
```

profile of v0, /device:TPU:1, one launch (start us, length us, event | category | flops | bytes accessed | tf_op | source)
XLA Modules:
  0.0 403.7 jit_solution(1863392339717188709)
XLA Ops:
  7.4 2.4 broadcast_in_dim.19
  9.7 10.2 %all-to-all-start = ((bf16[16,256,224]{1,2,0:T(8,128)(2,1)}), bf16[16,256,224]{1,2,0:T(8,128)(2,1)}, u32[]{:S(2)}, u32[]{:S(2)}) async-start(bf16[16,256,224]{1,2,0:T(8,128)(2,1)} %broadcast_in_dim.19), calls=%async_computation | async-start | bytes 3670016 | tf_op jit(solution)/shard_map/all_to_all | solution.py:12
  20.0 0.7 all-gather.3.cloned.1.call-update
  20.7 41.4 %all-to-all-done = bf16[16,256,224]{1,2,0:T(8,128)(2,1)} async-done(((bf16[16,256,224]{1,2,0:T(8,128)(2,1)}), bf16[16,256,224]{1,2,0:T(8,128)(2,1)}, u32[]{:S(2)}, u32[]{:S(2)}) %all-to-all-start) | async-done | bytes 1835040 | tf_op jit(solution)/shard_map/all_to_all | solution.py:12
  62.0 9.3 %all-to-all-start.1 = ((bf16[16,256,224]{1,2,0:T(8,128)(2,1)}), bf16[16,256,224]{1,2,0:T(8,128)(2,1)S(1)}, u32[]{:S(2)}, u32[]{:S(2)}) async-start(bf16[16,256,224]{1,2,0:T(8,128)(2,1)} %all-to-all-done), calls=%async_computation.1 | async-start | bytes 3670016 | tf_op jit(solution)/shard_map/all_to_all | solution.py:69
  71.3 7.7 %all-gather.3.cloned.1.call-done = bf16[256,3584]{0,1:T(8,128)(2,1)} async-done(((bf16[256,224]{0,1:T(8,128)(2,1)}), bf16[256,3584]{0,1:T(8,128)(2,1)}) %all-gather.3.cloned.1.call-update) | async-done | bytes 1835024 | tf_op jit(solution)/shard_map/all_gather | solution.py:70
  79.0 17.8 %all-to-all-done.1 = bf16[16,256,224]{1,2,0:T(8,128)(2,1)S(1)} async-done(((bf16[16,256,224]{1,2,0:T(8,128)(2,1)}), bf16[16,256,224]{1,2,0:T(8,128)(2,1)S(1)}, u32[]{:S(2)}, u32[]{:S(2)}) %all-to-all-start.1) | async-done | bytes 1835040 | tf_op jit(solution)/shard_map/all_to_all | solution.py:69
  96.9 2.4 fusion.2
  99.2 13.2 %all_to_all.43 = f32[16,1,256]{2,1,0:T(1,128)S(1)} all-to-all(f32[16,1,256]{2,1,0:T(1,128)S(1)} %broadcast_in_dim.20), channel_id=1, replica_groups=mesh['train'=16,'test'=16] {'test'}, dimensions={0} | all-to-all | bytes 32768 | tf_op jit(solution)/shard_map/all_to_all | solution.py:12
  112.4 0.8 broadcast_in_dim.22
  113.3 3.8 all-to-all-start.4
  117.2 11.1 %all-to-all-done.4 = bf16[16,224,64]{1,2,0:T(8,128)(2,1)S(1)} async-done(((bf16[16,224,64]{1,2,0:T(8,128)(2,1)}), bf16[16,224,64]{1,2,0:T(8,128)(2,1)S(1)}, u32[]{:S(2)}, u32[]{:S(2)}) %all-to-all-start.4) | async-done | bytes 458784 | tf_op jit(solution)/shard_map/all_to_all | solution.py:12
  128.9 4.5 %all-to-all-start.3 = ((f32[16,1,256]{2,1,0:T(1,128)}), f32[16,1,256]{2,1,0:T(1,128)S(1)}, u32[]{:S(2)}, u32[]{:S(2)}) async-start(f32[16,1,256]{2,1,0:T(1,128)} %broadcast_in_dim.21), calls=%async_computation.3 | async-start | bytes 32768 | tf_op jit(solution)/shard_map/all_to_all | solution.py:12
  133.4 1.1 copy.55
  134.5 1.9 reshape.84
  136.4 4.4 %all-to-all-done.3 = f32[16,1,256]{2,1,0:T(1,128)S(1)} async-done(((f32[16,1,256]{2,1,0:T(1,128)}), f32[16,1,256]{2,1,0:T(1,128)S(1)}, u32[]{:S(2)}, u32[]{:S(2)}) %all-to-all-start.3) | async-done | bytes 16416 | tf_op jit(solution)/shard_map/all_to_all | solution.py:12
  140.8 2.2 convolution_multiply_fusion
  143.1 2.0 convolution_dynamic-update-slice_fusion
  145.1 1.1 copy.72
  146.2 4.8 %all-to-all-start.5 = ((f32[16,256,64]{1,2,0:T(8,128)}), f32[16,256,64]{1,2,0:T(8,128)S(1)}, u32[]{:S(2)}, u32[]{:S(2)}) async-start(f32[16,256,64]{1,2,0:T(8,128)} %bitcast.26), calls=%async_computation.5 | async-start | bytes 2097152 | tf_op jit(solution)/shard_map/all_to_all | solution.py:43
  151.1 0.9 fusion.3
  152.0 1.0 reshape.82
  153.0 1.8 fusion.4
  154.7 1.6 reshape.83
  156.3 1.8 convolution_multiply_fusion.1
  158.1 1.8 fusion.5
  160.0 16.6 %all-to-all-done.5 = f32[16,256,64]{1,2,0:T(8,128)S(1)} async-done(((f32[16,256,64]{1,2,0:T(8,128)}), f32[16,256,64]{1,2,0:T(8,128)S(1)}, u32[]{:S(2)}, u32[]{:S(2)}) %all-to-all-start.5) | async-done | bytes 1048608 | tf_op jit(solution)/shard_map/all_to_all | solution.py:43
  176.9 0.7 pad_maximum_fusion
  178.2 208.8 %all-reduce.2.cloned.1.call-done = f32[65536]{0:T(1024)} async-done(((f32[65536]{0:T(1024)}), f32[65536]{0:T(1024)}) %all-reduce.2.cloned.1.call-update) | async-done | bytes 262160 | tf_op jit(solution)/shard_map/psum | solution.py:51
  387.0 1.0 fusion.1
  388.7 0.7 add_convert_fusion
  389.5 6.7 %fusion.6 = f32[256,1024]{1,0:T(8,128)} fusion(bf16[256,4096]{0,1:T(8,128)(2,1)S(1)} %bitcast.28, bf16[1024,4096]{1,0:T(8,128)(2,1)} %all-gather.5.cloned.1.call-done), kind=kOutput, calls=%fused_computation.17 | convolution fusion | flops 2147483648 | bytes 11534336 | tf_op jit(solution)/shard_map/dot_general | solution.py:113
  (47 shorter events, 2.6 us)
Async XLA Ops:
  7.4 143.7 %copy-start = (bf16[256,224]{0,1:T(8,128)(2,1)S(1)}, bf16[256,224]{0,1:T(8,128)(2,1)}, u32[]{:S(2)}) copy-start(bf16[256,224]{0,1:T(8,128)(2,1)} %param.10) | copy-start | bytes 344068
  9.7 52.3 %all-to-all-start = ((bf16[16,256,224]{1,2,0:T(8,128)(2,1)}), bf16[16,256,224]{1,2,0:T(8,128)(2,1)}, u32[]{:S(2)}, u32[]{:S(2)}) async-start(bf16[16,256,224]{1,2,0:T(8,128)(2,1)} %broadcast_in_dim.19), calls=%async_computation | async-start | bytes 3670016 | tf_op jit(solution)/shard_map/all_to_all | solution.py:12
  19.9 59.1 %all-gather.3.cloned.1.call-start = ((), (), s32[]{:S(2)}) async-start(), calls=%async_computation.6 | async-start | bytes 1949696 | tf_op jit(solution)/shard_map/all_gather | solution.py:70
  20.6 91.8 %copy-start.4 = (bf16[224,64]{0,1:T(8,128)(2,1)S(1)}, bf16[224,64]{0,1:T(8,128)(2,1)}, u32[]{:S(2)}) copy-start(bf16[224,64]{0,1:T(8,128)(2,1)} %param.16) | copy-start | bytes 86020
  62.0 34.8 %all-to-all-start.1 = ((bf16[16,256,224]{1,2,0:T(8,128)(2,1)}), bf16[16,256,224]{1,2,0:T(8,128)(2,1)S(1)}, u32[]{:S(2)}, u32[]{:S(2)}) async-start(bf16[16,256,224]{1,2,0:T(8,128)(2,1)} %all-to-all-done), calls=%async_computation.1 | async-start | bytes 3670016 | tf_op jit(solution)/shard_map/all_to_all | solution.py:69
  96.9 44.0 %copy-start.7 = (s32[256]{0:T(256)S(1)}, s32[256]{0:T(256)}, u32[]{:S(2)}) copy-start(s32[256]{0:T(256)} %param.14) | copy-start | bytes 3076
  99.2 43.8 %copy-start.1 = (f32[256,256]{0,1:T(8,128)}, f32[256,256]{0,1:T(8,128)S(1)}, u32[]{:S(2)}) copy-start(f32[256,256]{0,1:T(8,128)S(1)} %get-tuple-element.10) | copy-start | bytes 786436
  113.3 15.0 %all-to-all-start.4 = ((bf16[16,224,64]{1,2,0:T(8,128)(2,1)}), bf16[16,224,64]{1,2,0:T(8,128)(2,1)S(1)}, u32[]{:S(2)}, u32[]{:S(2)}) async-start(bf16[16,224,64]{1,2,0:T(8,128)(2,1)} %broadcast_in_dim.22), calls=%async_computation.4 | async-start | bytes 1048576 | tf_op jit(solution)/shard_map/all_to_all | solution.py:12
  117.1 26.0 %copy-start.5 = (f32[256]{0:T(256)}, f32[256]{0:T(256)S(1)}, u32[]{:S(2)}) copy-start(f32[256]{0:T(256)S(1)} %reduce_max.19) | copy-start | bytes 3076
  128.9 11.9 %all-to-all-start.3 = ((f32[16,1,256]{2,1,0:T(1,128)}), f32[16,1,256]{2,1,0:T(1,128)S(1)}, u32[]{:S(2)}, u32[]{:S(2)}) async-start(f32[16,1,256]{2,1,0:T(1,128)} %broadcast_in_dim.21), calls=%async_computation.3 | async-start | bytes 32768 | tf_op jit(solution)/shard_map/all_to_all | solution.py:12
  133.4 9.6 %copy-start.8 = (s32[256]{0:T(256)}, s32[256]{0:T(256)S(1)}, u32[]{:S(2)}) copy-start(s32[256]{0:T(256)S(1)} %iota_add_fusion) | copy-start | bytes 3076
  140.8 4.3 %copy-start.6 = (f32[256]{0:T(256)}, f32[256]{0:T(256)S(1)}, u32[]{:S(2)}) copy-start(f32[256]{0:T(256)S(1)} %reduce_sum.28) | copy-start | bytes 3076
  143.1 7.9 %copy-start.3 = (bf16[224,64]{0,1:T(8,128)(2,1)S(1)}, bf16[224,64]{0,1:T(8,128)(2,1)}, u32[]{:S(2)}) copy-start(bf16[224,64]{0,1:T(8,128)(2,1)} %param.15) | copy-start | bytes 86020
  146.2 30.4 %all-to-all-start.5 = ((f32[16,256,64]{1,2,0:T(8,128)}), f32[16,256,64]{1,2,0:T(8,128)S(1)}, u32[]{:S(2)}, u32[]{:S(2)}) async-start(f32[16,256,64]{1,2,0:T(8,128)} %bitcast.26), calls=%async_computation.5 | async-start | bytes 2097152 | tf_op jit(solution)/shard_map/all_to_all | solution.py:43
  151.0 235.9 %all-reduce.2.cloned.1.call-start = ((), (), s32[]{:S(2)}) async-start(), calls=%async_computation.7 | async-start | bytes 524288 | tf_op jit(solution)/shard_map/psum | solution.py:51
  158.1 18.7 %copy-start.2 = (f32[16384]{0:T(1024)S(1)}, f32[16384]{0:T(1024)}, u32[]{:S(2)}) copy-start(f32[16384]{0:T(1024)} %reshape.83) | copy-start | bytes 196612
  158.1 20.1 %copy-start.9 = (s32[256]{0:T(256)S(1)}, s32[256]{0:T(256)}, u32[]{:S(2)}) copy-start(s32[256]{0:T(256)} %param.13) | copy-start | bytes 3076
  177.6 211.9 %all-gather.5.cloned.1.call-start = ((), (), s32[]{:S(2)}) async-start(), calls=%async_computation.8 | async-start | bytes 8912896 | tf_op jit(solution)/shard_map/all_gather | solution.py:115
Sparse Core Ops, SparseCore 0:
  23.4 55.5 all-gather.2
  177.7 209.1 all-reduce.1
Sparse Core Ops, SparseCore 1:
  179.9 97.2 all-gather.4
where the time goes:
time: 404 us
  waiting for transfers between devices  309 us (76%)
  starting transfers between devices  32.9 us (8%)
  matrix products  19.4 us (5%)
  between operations  15.2 us (4%)
  blocking collectives  13.2 us (3%)
  local copies, waits for them, and re-layouts  12.5 us (3%)
    psum x1, waiting for transfers between devices, in_one(): so_far = lax.psum(jnp.concatenate([a.ravel() for a in arrays]), axis)  209 us
    all_to_all x3, waiting for transfers between devices, copy_for_each(): return lax.all_to_all(copies, axis, split_axis=0, concat_axis=0, tiled=True)  56.9 us
    all_to_all x3, starting transfers between devices, copy_for_each(): return lax.all_to_all(copies, axis, split_axis=0, concat_axis=0, tiled=True)  18.4 us
    all_to_all x1, waiting for transfers between devices, local(): lax.all_to_all(whole_pass, 'test', split_axis=0, concat_axis=1, tiled=True)  17.8 us
    all_to_all x1, waiting for transfers between devices, summed_on_arrival(): blocks = lax.all_to_all(split_up(value, dim, count), axis, 0, 0, tiled=True)  16.6 us
    all_to_all x1, blocking collectives, copy_for_each(): return lax.all_to_all(copies, axis, split_axis=0, concat_axis=0, tiled=True)  13.2 us
    all_to_all x1, starting transfers between devices, local(): lax.all_to_all(whole_pass, 'test', split_axis=0, concat_axis=1, tiled=True)  9.32 us
  transfers between devices with their start and end apart: 8, of which 7 were waited for; matrix products, arithmetic and copies ran while one was open for 4% of the time, Pallas kernels for 0%

commit v1 on v0

--- a/solution.py
+++ b/solution.py
@@ -48,7 +48,9 @@
     ends = [0]
     for a in arrays:
         ends.append(ends[-1] + a.size)
-    so_far = lax.psum(jnp.concatenate([a.ravel() for a in arrays]), axis)
+    x = jnp.concatenate([a.ravel() for a in arrays])
+    parts = lax.all_gather(x, axis)
+    so_far = jnp.sum(parts, axis=0)
     return tuple((so_far[b:e].reshape(a.shape) for a, b, e in zip(arrays, ends, ends[1:])))
 
 

time: 404 us -> 350 us (0.87)
  waiting for transfers between devices: 309 us -> 250 us
    psum x1 -> x0, waiting for transfers between devices: 209 us -> none  [in_one(): so_far = lax.psum(jnp.concatenate([a.ravel() for a in arrays]), axis)]
    all_gather x1, waiting for transfers between devices: 0.03 us -> 92.7 us  [local(): lax.all_gather(test_grads, 'train', axis=0, tiled=True)]
    all_gather x0 -> x1, waiting for transfers between devices: none -> 57.2 us  [in_one(): parts = lax.all_gather(x, axis)]
  transfers between devices with their start and end apart: 8 -> 8, of which waited for: 7 -> 8; matrix products, arithmetic and copies ran while one was open for 4% -> 6% of each run, Pallas kernels for 0% -> 0%
where the time goes in v1:
time: 350 us; the launch traced here: 349 us
  waiting for transfers between devices  250 us (71%)
  starting transfers between devices  32.9 us (9%)
  matrix products  19.4 us (6%)
  local copies, waits for them, and re-layouts  15.4 us (4%)
  between operations  13.4 us (4%)
  blocking collectives  13.2 us (4%)
  other arithmetic  4.66 us (1%)
    all_gather x1, waiting for transfers between devices, local(): lax.all_gather(test_grads, 'train', axis=0, tiled=True)  92.7 us
    all_gather x1, waiting for transfers between devices, in_one(): parts = lax.all_gather(x, axis)  57.2 us
    all_to_all x3, waiting for transfers between devices, copy_for_each(): return lax.all_to_all(copies, axis, split_axis=0, concat_axis=0, tiled=True)  56.9 us
    all_to_all x3, starting transfers between devices, copy_for_each(): return lax.all_to_all(copies, axis, split_axis=0, concat_axis=0, tiled=True)  18.4 us
    all_to_all x1, waiting for transfers between devices, local(): lax.all_to_all(whole_pass, 'test', split_axis=0, concat_axis=1, tiled=True)  17.8 us
    all_to_all x1, waiting for transfers between devices, summed_on_arrival(): blocks = lax.all_to_all(split_up(value, dim, count), axis, 0, 0, tiled=True)  16.6 us
    all_to_all x1, blocking collectives, copy_for_each(): return lax.all_to_all(copies, axis, split_axis=0, concat_axis=0, tiled=True)  13.2 us
    all_to_all x1, starting transfers between devices, local(): lax.all_to_all(whole_pass, 'test', split_axis=0, concat_axis=1, tiled=True)  9.32 us
  transfers between devices with their start and end apart: 8, of which 8 were waited for; matrix products, arithmetic and copies ran while one was open for 6% of the time, Pallas kernels for 0%

profile of v1, /device:TPU:1, one launch (start us, length us, event | category | flops | bytes accessed | tf_op | source)
XLA Modules:
  0.0 349.0 jit_solution(6144359740920412831)
XLA Ops:
  6.5 2.4 broadcast_in_dim.19
  8.9 10.2 %all-to-all-start = ((bf16[16,256,224]{1,2,0:T(8,128)(2,1)}), bf16[16,256,224]{1,2,0:T(8,128)(2,1)}, u32[]{:S(2)}, u32[]{:S(2)}) async-start(bf16[16,256,224]{1,2,0:T(8,128)(2,1)} %broadcast_in_dim.19), calls=%async_computation | async-start | bytes 3670016 | tf_op jit(solution)/shard_map/all_to_all | solution.py:12
  19.8 41.4 %all-to-all-done = bf16[16,256,224]{1,2,0:T(8,128)(2,1)} async-done(((bf16[16,256,224]{1,2,0:T(8,128)(2,1)}), bf16[16,256,224]{1,2,0:T(8,128)(2,1)}, u32[]{:S(2)}, u32[]{:S(2)}) %all-to-all-start) | async-done | bytes 1835040 | tf_op jit(solution)/shard_map/all_to_all | solution.py:12
  61.2 9.3 %all-to-all-start.1 = ((bf16[16,256,224]{1,2,0:T(8,128)(2,1)}), bf16[16,256,224]{1,2,0:T(8,128)(2,1)S(1)}, u32[]{:S(2)}, u32[]{:S(2)}) async-start(bf16[16,256,224]{1,2,0:T(8,128)(2,1)} %all-to-all-done), calls=%async_computation.1 | async-start | bytes 3670016 | tf_op jit(solution)/shard_map/all_to_all | solution.py:71
  70.5 7.7 %all-gather.5.cloned.1.call-done = bf16[256,3584]{0,1:T(8,128)(2,1)} async-done(((bf16[256,224]{0,1:T(8,128)(2,1)}), bf16[256,3584]{0,1:T(8,128)(2,1)}) %all-gather.5.cloned.1.call-update) | async-done | bytes 1835024 | tf_op jit(solution)/shard_map/all_gather | solution.py:72
  78.2 17.8 %all-to-all-done.1 = bf16[16,256,224]{1,2,0:T(8,128)(2,1)S(1)} async-done(((bf16[16,256,224]{1,2,0:T(8,128)(2,1)}), bf16[16,256,224]{1,2,0:T(8,128)(2,1)S(1)}, u32[]{:S(2)}, u32[]{:S(2)}) %all-to-all-start.1) | async-done | bytes 1835040 | tf_op jit(solution)/shard_map/all_to_all | solution.py:71
  96.0 2.4 fusion.2
  98.4 13.2 %all_to_all.43 = f32[16,1,256]{2,1,0:T(1,128)S(1)} all-to-all(f32[16,1,256]{2,1,0:T(1,128)S(1)} %broadcast_in_dim.20), channel_id=1, replica_groups=mesh['train'=16,'test'=16] {'test'}, dimensions={0} | all-to-all | bytes 32768 | tf_op jit(solution)/shard_map/all_to_all | solution.py:12
  111.6 0.8 broadcast_in_dim.22
  112.5 3.8 %all-to-all-start.4 = ((bf16[16,224,64]{1,2,0:T(8,128)(2,1)}), bf16[16,224,64]{1,2,0:T(8,128)(2,1)S(1)}, u32[]{:S(2)}, u32[]{:S(2)}) async-start(bf16[16,224,64]{1,2,0:T(8,128)(2,1)} %broadcast_in_dim.22), calls=%async_computation.4 | async-start | bytes 1048576 | tf_op jit(solution)/shard_map/all_to_all | solution.py:12
  116.3 11.1 %all-to-all-done.4 = bf16[16,224,64]{1,2,0:T(8,128)(2,1)S(1)} async-done(((bf16[16,224,64]{1,2,0:T(8,128)(2,1)}), bf16[16,224,64]{1,2,0:T(8,128)(2,1)S(1)}, u32[]{:S(2)}, u32[]{:S(2)}) %all-to-all-start.4) | async-done | bytes 458784 | tf_op jit(solution)/shard_map/all_to_all | solution.py:12
  128.1 4.5 %all-to-all-start.3 = ((f32[16,1,256]{2,1,0:T(1,128)}), f32[16,1,256]{2,1,0:T(1,128)S(1)}, u32[]{:S(2)}, u32[]{:S(2)}) async-start(f32[16,1,256]{2,1,0:T(1,128)} %broadcast_in_dim.21), calls=%async_computation.3 | async-start | bytes 32768 | tf_op jit(solution)/shard_map/all_to_all | solution.py:12
  132.6 1.1 copy.55
  133.7 1.9 reshape.84
  135.6 4.4 %all-to-all-done.3 = f32[16,1,256]{2,1,0:T(1,128)S(1)} async-done(((f32[16,1,256]{2,1,0:T(1,128)}), f32[16,1,256]{2,1,0:T(1,128)S(1)}, u32[]{:S(2)}, u32[]{:S(2)}) %all-to-all-start.3) | async-done | bytes 16416 | tf_op jit(solution)/shard_map/all_to_all | solution.py:12
  140.0 2.2 convolution_multiply_fusion
  142.3 2.0 convolution_dynamic-update-slice_fusion
  144.3 1.1 copy.72
  145.4 4.8 %all-to-all-start.5 = ((f32[16,256,64]{1,2,0:T(8,128)}), f32[16,256,64]{1,2,0:T(8,128)S(1)}, u32[]{:S(2)}, u32[]{:S(2)}) async-start(f32[16,256,64]{1,2,0:T(8,128)} %bitcast.26), calls=%async_computation.5 | async-start | bytes 2097152 | tf_op jit(solution)/shard_map/all_to_all | solution.py:43
  150.3 0.9 fusion.3
  151.1 1.0 reshape.82
  152.1 1.8 fusion.4
  153.9 1.6 reshape.83
  155.5 1.8 convolution_multiply_fusion.1
  157.3 1.8 fusion.5
  159.2 16.6 %all-to-all-done.5 = f32[16,256,64]{1,2,0:T(8,128)S(1)} async-done(((f32[16,256,64]{1,2,0:T(8,128)}), f32[16,256,64]{1,2,0:T(8,128)S(1)}, u32[]{:S(2)}, u32[]{:S(2)}) %all-to-all-start.5) | async-done | bytes 1048608 | tf_op jit(solution)/shard_map/all_to_all | solution.py:43
  177.5 57.2 %all-gather.9.cloned.1.call-done = f32[1048576]{0:T(1024)} async-done(((f32[65536]{0:T(1024)}), f32[1048576]{0:T(1024)}) %all-gather.9.cloned.1.call-update) | async-done | bytes 4194320 | tf_op jit(solution)/shard_map/all_gather | solution.py:52
  234.7 3.9 %reshape.88 = f32[16,65536]{1,0:T(8,128)} reshape(f32[1048576]{0:T(1024)} %all-gather.9.cloned.1.call-done) | data formatting | bytes 8388608 | tf_op jit(solution)/shard_map/all_gather | solution.py:52
  238.6 2.9 reduce_sum.39
  242.4 0.7 add_convert_fusion
  243.1 92.7 %all-gather.7.cloned.1.call-done = bf16[1024,4096]{1,0:T(8,128)(2,1)} async-done(((bf16[64,4096]{1,0:T(8,128)(2,1)}), bf16[1024,4096]{1,0:T(8,128)(2,1)}) %all-gather.7.cloned.1.call-update) | async-done | bytes 8388624 | tf_op jit(solution)/shard_map/all_gather | solution.py:117
  335.8 6.7 %fusion.6 = f32[256,1024]{1,0:T(8,128)} fusion(bf16[256,4096]{0,1:T(8,128)(2,1)S(1)} %bitcast.28, bf16[1024,4096]{1,0:T(8,128)(2,1)} %all-gather.7.cloned.1.call-done), kind=kOutput, calls=%fused_computation.17 | convolution fusion | flops 2147483648 | bytes 11534336 | tf_op jit(solution)/shard_map/dot_general | solution.py:115
  (49 shorter events, 4.2 us)
Async XLA Ops:
  6.5 143.7 %copy-start = (bf16[256,224]{0,1:T(8,128)(2,1)S(1)}, bf16[256,224]{0,1:T(8,128)(2,1)}, u32[]{:S(2)}) copy-start(bf16[256,224]{0,1:T(8,128)(2,1)} %param.10) | copy-start | bytes 344068
  8.9 52.3 %all-to-all-start = ((bf16[16,256,224]{1,2,0:T(8,128)(2,1)}), bf16[16,256,224]{1,2,0:T(8,128)(2,1)}, u32[]{:S(2)}, u32[]{:S(2)}) async-start(bf16[16,256,224]{1,2,0:T(8,128)(2,1)} %broadcast_in_dim.19), calls=%async_computation | async-start | bytes 3670016 | tf_op jit(solution)/shard_map/all_to_all | solution.py:12
  19.1 59.1 %all-gather.5.cloned.1.call-start = ((), (), s32[]{:S(2)}) async-start(), calls=%async_computation.6 | async-start | bytes 1949696 | tf_op jit(solution)/shard_map/all_gather | solution.py:72
  19.8 91.8 %copy-start.4 = (bf16[224,64]{0,1:T(8,128)(2,1)S(1)}, bf16[224,64]{0,1:T(8,128)(2,1)}, u32[]{:S(2)}) copy-start(bf16[224,64]{0,1:T(8,128)(2,1)} %param.16) | copy-start | bytes 86020
  61.2 34.8 %all-to-all-start.1 = ((bf16[16,256,224]{1,2,0:T(8,128)(2,1)}), bf16[16,256,224]{1,2,0:T(8,128)(2,1)S(1)}, u32[]{:S(2)}, u32[]{:S(2)}) async-start(bf16[16,256,224]{1,2,0:T(8,128)(2,1)} %all-to-all-done), calls=%async_computation.1 | async-start | bytes 3670016 | tf_op jit(solution)/shard_map/all_to_all | solution.py:71
  96.0 44.0 %copy-start.7 = (s32[256]{0:T(256)S(1)}, s32[256]{0:T(256)}, u32[]{:S(2)}) copy-start(s32[256]{0:T(256)} %param.14) | copy-start | bytes 3076
  98.4 43.8 %copy-start.1 = (f32[256,256]{0,1:T(8,128)}, f32[256,256]{0,1:T(8,128)S(1)}, u32[]{:S(2)}) copy-start(f32[256,256]{0,1:T(8,128)S(1)} %get-tuple-element.10) | copy-start | bytes 786436
  112.5 15.0 %all-to-all-start.4 = ((bf16[16,224,64]{1,2,0:T(8,128)(2,1)}), bf16[16,224,64]{1,2,0:T(8,128)(2,1)S(1)}, u32[]{:S(2)}, u32[]{:S(2)}) async-start(bf16[16,224,64]{1,2,0:T(8,128)(2,1)} %broadcast_in_dim.22), calls=%async_computation.4 | async-start | bytes 1048576 | tf_op jit(solution)/shard_map/all_to_all | solution.py:12
  116.2 26.0 %copy-start.5 = (f32[256]{0:T(256)}, f32[256]{0:T(256)S(1)}, u32[]{:S(2)}) copy-start(f32[256]{0:T(256)S(1)} %reduce_max.19) | copy-start | bytes 3076
  128.1 11.9 %all-to-all-start.3 = ((f32[16,1,256]{2,1,0:T(1,128)}), f32[16,1,256]{2,1,0:T(1,128)S(1)}, u32[]{:S(2)}, u32[]{:S(2)}) async-start(f32[16,1,256]{2,1,0:T(1,128)} %broadcast_in_dim.21), calls=%async_computation.3 | async-start | bytes 32768 | tf_op jit(solution)/shard_map/all_to_all | solution.py:12
  132.6 9.6 %copy-start.8 = (s32[256]{0:T(256)}, s32[256]{0:T(256)S(1)}, u32[]{:S(2)}) copy-start(s32[256]{0:T(256)S(1)} %iota_add_fusion) | copy-start | bytes 3076
  140.0 4.3 %copy-start.6 = (f32[256]{0:T(256)}, f32[256]{0:T(256)S(1)}, u32[]{:S(2)}) copy-start(f32[256]{0:T(256)S(1)} %reduce_sum.37) | copy-start | bytes 3076
  142.3 7.9 %copy-start.3 = (bf16[224,64]{0,1:T(8,128)(2,1)S(1)}, bf16[224,64]{0,1:T(8,128)(2,1)}, u32[]{:S(2)}) copy-start(bf16[224,64]{0,1:T(8,128)(2,1)} %param.15) | copy-start | bytes 86020
  145.4 30.4 %all-to-all-start.5 = ((f32[16,256,64]{1,2,0:T(8,128)}), f32[16,256,64]{1,2,0:T(8,128)S(1)}, u32[]{:S(2)}, u32[]{:S(2)}) async-start(f32[16,256,64]{1,2,0:T(8,128)} %bitcast.26), calls=%async_computation.5 | async-start | bytes 2097152 | tf_op jit(solution)/shard_map/all_to_all | solution.py:43
  150.2 84.5 %all-gather.9.cloned.1.call-start = ((), (), s32[]{:S(2)}) async-start(), calls=%async_computation.8 | async-start | bytes 4456448 | tf_op jit(solution)/shard_map/all_gather | solution.py:52
  157.3 18.7 %copy-start.2 = (f32[16384]{0:T(1024)S(1)}, f32[16384]{0:T(1024)}, u32[]{:S(2)}) copy-start(f32[16384]{0:T(1024)} %reshape.83) | copy-start | bytes 196612
  157.3 20.2 %copy-start.9 = (s32[256]{0:T(256)S(1)}, s32[256]{0:T(256)}, u32[]{:S(2)}) copy-start(s32[256]{0:T(256)} %param.13) | copy-start | bytes 3076
  176.8 159.0 %all-gather.7.cloned.1.call-start = ((), (), s32[]{:S(2)}) async-start(), calls=%async_computation.7 | async-start | bytes 8912896 | tf_op jit(solution)/shard_map/all_gather | solution.py:117
Sparse Core Ops, SparseCore 0:
  22.6 55.5 all-gather.4
  176.9 57.8 all-gather.8
  236.5 99.1 all-gather.6
